TPU v7x, 32 devices: a whole 2x2x4 slice. The times are simulated.
32 devices in a mesh: slab: 2 (over y), date: 4 (over z), rng: 2 (over x), az: 2 (over core).
Axes of the slice: x: 2, y: 2, z: 4, core: 2. Of those that a mesh axis runs over, the one named last changes fastest.
Arguments:
- slc: bfloat16 [64, 2, 128, 512], P(('slab', 'date'), None, 'az', 'rng'), parts along dimension 0, may hold values from -30 to 30
- lags: int32 [32, 6], P('date'), may hold values from 0 to 8, as said below
Outputs:
- coherence: bfloat16 [64, 6, 128, 512], P(('slab', 'date'), None, 'az', 'rng'), parts along dimension 0
- log_ratio: bfloat16 [64, 6, 128, 512], P(('slab', 'date'), None, 'az', 'rng'), parts along dimension 0
- quegan: float32 [64, 128, 512], P(('slab', 'date'), 'az', 'rng'), parts along dimension 0
There are 2 independent parts, one for each index of `slab`. A program takes and returns all parts, laid end to end along the dimension named above; an argument that names none is the same for every part. Nothing has to cross between parts.
Inputs may be any that keep to these rules, and one draw needn't show every extreme that they name: Each entry is 0 (no partner) or a lag with date + lag < 32; the nonzero lags of one date are distinct; date 0 lists 6 partners, one of them at lag 8.
All inputs are finite; a program needn't handle non-finite values.
Results may differ from a plain program's by a relative error of at most 0.012.
Values may be sent and summed in bfloat16 or wider, within the bound.
A program may use at most 64 MiB of HBM per device.

v0:
```python
import jax
import jax.numpy as jnp
from jax import lax
from jax.sharding import PartitionSpec as P

HALF_AZ = 2
HALF_RG = 10


EPS = 1e-05


def shifted(x, axis, by):
    devices = lax.axis_size(axis)
    pairs = [(i, i + by) for i in range(devices) if 0 <= i + by < devices]
    return lax.ppermute(x, axis, pairs)


def with_halo(cells, sides, width):
    for axis, dim in sides:
        count = lax.axis_size(axis)
        ends = count - 1
        head = lax.slice_in_dim(cells, 0, width, axis=dim)
        tail = lax.slice_in_dim(cells, cells.shape[dim] - width, cells.shape[dim], axis=dim)
        cells = jnp.concatenate(
            [
                lax.ppermute(tail, axis, [(i, (i + 1) % count) for i in range(ends)]),
                cells,
                lax.ppermute(head, axis, [((i + 1) % count, i) for i in range(ends)]),
            ],
            axis=dim,
        )
    return cells


def box_mean(rimmed, band_matrix, line_count):
    row_sums = rimmed[..., 0:line_count, :]
    for offset in range(1, 2 * HALF_AZ + 1):
        row_sums = row_sums + rimmed[..., offset : offset + line_count, :]
    totals = jnp.einsum(
        "...c,cj->...j",
        row_sums,
        band_matrix,
        precision=lax.Precision.HIGHEST,
        preferred_element_type=jnp.float32,
    )
    return totals / float((2 * HALF_AZ + 1) * (2 * HALF_RG + 1))


def on_device(slc, lags):
    date_count = slc.shape[0]
    line_count = slc.shape[2]
    column_count = slc.shape[3]
    later_tiles = shifted(slc, "date", -1)
    tiles = jnp.concatenate([slc, later_tiles], axis=0)
    tiles = with_halo(tiles, (("az", 2),), HALF_AZ)
    tiles = with_halo(tiles, (("rng", 3),), HALF_RG)
    column_in = jnp.arange(column_count + 2 * HALF_RG, dtype=jnp.int32)[:, None]
    column_out = jnp.arange(column_count, dtype=jnp.int32)[None, :]
    band_matrix = ((column_in >= column_out) & (column_in <= column_out + 2 * HALF_RG)).astype(
        jnp.float32
    )
    real_part = tiles[:, 0].astype(jnp.float32)
    imag_part = tiles[:, 1].astype(jnp.float32)
    powers = real_part**2 + imag_part**2
    mean_power = box_mean(powers, band_matrix, line_count) + EPS
    own_power = powers[
        :date_count, HALF_AZ : HALF_AZ + line_count, HALF_RG : HALF_RG + column_count
    ]
    own_mean = mean_power[:date_count]
    local_sum = jnp.sum(own_power / own_mean, axis=0)
    totals = lax.psum(local_sum.astype(jnp.bfloat16), "date").astype(jnp.float32)
    quegan = own_mean * totals / float(date_count * lax.axis_size("date"))

    def one_date(packed):
        date_index, lag_row = packed
        live_slots = lag_row > 0
        partners = date_index + jnp.where(live_slots, lag_row, 0)
        own_tile = tiles[date_index].astype(jnp.float32)
        second = jnp.take(tiles, partners, axis=0).astype(jnp.float32)
        cross_re = own_tile[0][None] * second[:, 0] + own_tile[1][None] * second[:, 1]
        cross_im = own_tile[1][None] * second[:, 0] - own_tile[0][None] * second[:, 1]
        boxed_cross = box_mean(jnp.stack([cross_re, cross_im]), band_matrix, line_count)
        date_mean = mean_power[date_index][None]
        partner_mean = jnp.take(mean_power, partners, axis=0)
        coherence = (boxed_cross[0] ** 2 + boxed_cross[1] ** 2) / (date_mean * partner_mean)
        log_ratio = jnp.log(date_mean / partner_mean)
        slot_mask = live_slots[:, None, None]
        return (
            jnp.where(slot_mask, coherence, 0.0).astype(jnp.bfloat16),
            jnp.where(slot_mask, log_ratio, 0.0).astype(jnp.bfloat16),
        )

    coherence, log_ratio = lax.map(one_date, (jnp.arange(date_count, dtype=jnp.int32), lags))
    return (coherence, log_ratio, quegan)


def solution(mesh):
    return jax.shard_map(
        on_device,
        mesh=mesh,
        in_specs=(P(("slab", "date"), None, "az", "rng"), P("date", None)),
        out_specs=(
            P(("slab", "date"), None, "az", "rng"),
            P(("slab", "date"), None, "az", "rng"),
            P(("slab", "date"), "az", "rng"),
        ),
        check_vma=False,
    )
```

profile of v0, /device:TPU:0, one launch (start us, length us, event | category | flops | bytes accessed | tf_op | source)
XLA Modules:
  0.0 152.9 jit_solution(13524142023297033551)
XLA Ops:
  0.6 1.2 fusion.41
  1.8 1.3 collective-permute-start
  3.1 15.6 %collective-permute-done = bf16[8,2,64,256]{3,2,0,1:T(8,128)(2,1)S(1)} collective-permute-done((bf16[8,2,64,256]{3,2,0,1:T(8,128)(2,1)S(1)}, bf16[8,2,64,256]{3,2,0,1:T(8,128)(2,1)S(1)}, u32[]{:S(2)}, u32[]{:S(2)}) %collective-permute-start) | collective-permute-done | bytes 524320 | tf_op jit(solution)/shard_map/ppermute | solution.py:16
  18.8 1.3 collective-permute-start.1
  20.1 1.3 collective-permute-start.2
  21.4 1.8 %collective-permute-done.2 = bf16[16,2,2,256]{3,2,0,1:T(2,128)(2,1)S(1)} collective-permute-done((bf16[16,2,2,256]{3,2,0,1:T(2,128)(2,1)S(1)}, bf16[16,2,2,256]{3,2,0,1:T(2,128)(2,1)S(1)}, u32[]{:S(2)}, u32[]{:S(2)}) %collective-permute-start.2) | collective-permute-done | bytes 32800 | tf_op jit(solution)/shard_map/ppermute | solution.py:29
  24.9 1.3 collective-permute-start.4
  26.2 4.6 %collective-permute-start.3 = (bf16[16,2,68,10]{2,0,3,1:T(8,128)(2,1)S(1)}, bf16[16,2,68,10]{2,0,3,1:T(8,128)(2,1)S(1)}, u32[]{:S(2)}, u32[]{:S(2)}) collective-permute-start(bf16[16,2,68,10]{2,0,3,1:T(8,128)(2,1)S(1)} %copy.12), channel_id=1, source_target_pairs={{0,2},{1,3},{4,6},{5,7},{8,10},{9,11},{12,14},{13,15},{16,18},{17,... | collective-permute-start | bytes 130568 | tf_op jit(solution)/shard_map/ppermute | solution.py:27
  30.8 2.0 %collective-permute-done.3 = bf16[16,2,68,10]{2,0,3,1:T(8,128)(2,1)S(1)} collective-permute-done((bf16[16,2,68,10]{2,0,3,1:T(8,128)(2,1)S(1)}, bf16[16,2,68,10]{2,0,3,1:T(8,128)(2,1)S(1)}, u32[]{:S(2)}, u32[]{:S(2)}) %collective-permute-start.3) | collective-permute-done | bytes 43552 | tf_op jit(solution)/shard_map/ppermute | solution.py:27
  33.6 1.6 %pad_maximum_fusion.2 = bf16[16,2,68,276]{3,2,0,1:T(8,128)(2,1)S(1)} fusion(bf16[16,2,68,10]{3,2,0,1:T(8,128)(2,1)S(1)} %copy.15, bf16[16,2,2,256]{3,2,0,1:T(2,128)(2,1)S(1)} %collective-permute-done.2, bf16[16,2,64,256]{3,2,0,1:T(8,128)(2,1)S(1)} %constant_dynamic-update-slice_fusion, bf16[16,2,2,256]{3,2,0,1:T(2,128)(2,1)S(1)} %collective-permute-done.1, ...), kind=kLoop, calls=%fused_computation.59 | loop fusion | flops 6005760 | bytes 2402304 | tf_op jit(solution)/shard_map/concatenate | solution.py:25
  35.7 2.6 %fusion.33 = f32[16,64,256]{2,1,0:T(8,128)} fusion(f32[16,68,276]{2,1,0:T(8,128)S(1)} %add_bitcast_fusion, s32[256]{0:T(256)S(1)} %iota_add_fusion), kind=kOutput, calls=%fused_computation.68 | convolution fusion | flops 870087680 | bytes 8913920 | tf_op jit(solution)/shard_map/...c,cj->...j/dot_general | solution.py:40
  38.2 1.3 fusion.34
  39.5 17.4 %psum.7 = bf16[64,256]{1,0:T(8,128)(2,1)S(1)} all-reduce(bf16[64,256]{1,0:T(8,128)(2,1)S(1)} %fusion.34), channel_id=1, replica_groups=mesh['slab'=2,'date'=4,'rng'=2,'az'=2] {'date'}, use_global_device_ids=true, to_apply=%region_3.4 | all-reduce | flops 16384 | bytes 65536 | tf_op jit(solution)/shard_map/psum | solution.py:72
  56.9 94.1 %while.13 = (s32[]{:T(128)}, bf16[8,6,64,256]{3,2,1,0:T(8,128)(2,1)}, bf16[8,6,64,256]{3,2,1,0:T(8,128)(2,1)}, s32[8,6]{1,0:T(8,128)}, s32[8]{0:T(128)S(1)}, /*i...) while((s32[]{:T(128)}, ...), condition=%wide.region_1.0_spmd.clone, body=%wide.region_0.0_spmd.clone.sunk | while | flops 655798720 | bytes 8978221 | solution.py:94
  59.4 1.3 fusion.48
  60.7 1.3 bitcast_compare_fusion.2
  63.0 1.8 %gather_fusion = f32[6,64,256]{2,1,0:T(8,128)S(1)} fusion(f32[16,64,256]{2,1,0:T(8,128)} %get-tuple-element.206, s32[1024]{0:T(1024)S(1)} %pad_clamp_fusion.2), kind=kCustom, calls=%fused_computation.1.clone.clone.1 | custom fusion | bytes 786456 | tf_op jit(solution)/shard_map/while/body/eval_jaxpr/jit(_take)/gather | solution.py:85
  65.8 1.9 %convolution_multiply_fusion.2 = f32[2,6,64,256]{3,2,1,0:T(8,128)S(1)} fusion(f32[1,6,68,276]{3,2,1,0:T(8,128)S(1)} %get-tuple-element.174, f32[1,6,68,276]{3,2,1,0:T(8,128)S(1)} %get-tuple-element.175, s32[256]{0:T(256)S(1)} %get-tuple-element.207), kind=kOutput, calls=%fused_computation.11.clone.1 | convolution fusion | flops 653552640 | bytes 1688320 | tf_op jit(solution)/shard_map/while/body/eval_jaxpr/...c,cj->...j/dot_general | solution.py:40
  71.2 1.3 fusion.48
  72.5 1.3 bitcast_compare_fusion.2
  74.7 1.8 %gather_fusion = f32[6,64,256]{2,1,0:T(8,128)S(1)} fusion(f32[16,64,256]{2,1,0:T(8,128)} %get-tuple-element.206, s32[1024]{0:T(1024)S(1)} %pad_clamp_fusion.2), kind=kCustom, calls=%fused_computation.1.clone.clone.1 | custom fusion | bytes 786456 | tf_op jit(solution)/shard_map/while/body/eval_jaxpr/jit(_take)/gather | solution.py:85
  77.6 1.9 %convolution_multiply_fusion.2 = f32[2,6,64,256]{3,2,1,0:T(8,128)S(1)} fusion(f32[1,6,68,276]{3,2,1,0:T(8,128)S(1)} %get-tuple-element.174, f32[1,6,68,276]{3,2,1,0:T(8,128)S(1)} %get-tuple-element.175, s32[256]{0:T(256)S(1)} %get-tuple-element.207), kind=kOutput, calls=%fused_computation.11.clone.1 | convolution fusion | flops 653552640 | bytes 1688320 | tf_op jit(solution)/shard_map/while/body/eval_jaxpr/...c,cj->...j/dot_general | solution.py:40
  79.4 1.0 fusion.49
  82.9 1.3 fusion.48
  84.3 1.3 bitcast_compare_fusion.2
  86.5 1.8 %gather_fusion = f32[6,64,256]{2,1,0:T(8,128)S(1)} fusion(f32[16,64,256]{2,1,0:T(8,128)} %get-tuple-element.206, s32[1024]{0:T(1024)S(1)} %pad_clamp_fusion.2), kind=kCustom, calls=%fused_computation.1.clone.clone.1 | custom fusion | bytes 786456 | tf_op jit(solution)/shard_map/while/body/eval_jaxpr/jit(_take)/gather | solution.py:85
  89.3 1.9 %convolution_multiply_fusion.2 = f32[2,6,64,256]{3,2,1,0:T(8,128)S(1)} fusion(f32[1,6,68,276]{3,2,1,0:T(8,128)S(1)} %get-tuple-element.174, f32[1,6,68,276]{3,2,1,0:T(8,128)S(1)} %get-tuple-element.175, s32[256]{0:T(256)S(1)} %get-tuple-element.207), kind=kOutput, calls=%fused_computation.11.clone.1 | convolution fusion | flops 653552640 | bytes 1688320 | tf_op jit(solution)/shard_map/while/body/eval_jaxpr/...c,cj->...j/dot_general | solution.py:40
  94.7 1.3 fusion.48
  96.0 1.3 bitcast_compare_fusion.2
  98.2 1.8 %gather_fusion = f32[6,64,256]{2,1,0:T(8,128)S(1)} fusion(f32[16,64,256]{2,1,0:T(8,128)} %get-tuple-element.206, s32[1024]{0:T(1024)S(1)} %pad_clamp_fusion.2), kind=kCustom, calls=%fused_computation.1.clone.clone.1 | custom fusion | bytes 786456 | tf_op jit(solution)/shard_map/while/body/eval_jaxpr/jit(_take)/gather | solution.py:85
  101.1 1.9 %convolution_multiply_fusion.2 = f32[2,6,64,256]{3,2,1,0:T(8,128)S(1)} fusion(f32[1,6,68,276]{3,2,1,0:T(8,128)S(1)} %get-tuple-element.174, f32[1,6,68,276]{3,2,1,0:T(8,128)S(1)} %get-tuple-element.175, s32[256]{0:T(256)S(1)} %get-tuple-element.207), kind=kOutput, calls=%fused_computation.11.clone.1 | convolution fusion | flops 653552640 | bytes 1688320 | tf_op jit(solution)/shard_map/while/body/eval_jaxpr/...c,cj->...j/dot_general | solution.py:40
  106.5 1.3 fusion.48
  107.8 1.3 bitcast_compare_fusion.2
  110.0 1.8 %gather_fusion = f32[6,64,256]{2,1,0:T(8,128)S(1)} fusion(f32[16,64,256]{2,1,0:T(8,128)} %get-tuple-element.206, s32[1024]{0:T(1024)S(1)} %pad_clamp_fusion.2), kind=kCustom, calls=%fused_computation.1.clone.clone.1 | custom fusion | bytes 786456 | tf_op jit(solution)/shard_map/while/body/eval_jaxpr/jit(_take)/gather | solution.py:85
  112.8 1.9 %convolution_multiply_fusion.2 = f32[2,6,64,256]{3,2,1,0:T(8,128)S(1)} fusion(f32[1,6,68,276]{3,2,1,0:T(8,128)S(1)} %get-tuple-element.174, f32[1,6,68,276]{3,2,1,0:T(8,128)S(1)} %get-tuple-element.175, s32[256]{0:T(256)S(1)} %get-tuple-element.207), kind=kOutput, calls=%fused_computation.11.clone.1 | convolution fusion | flops 653552640 | bytes 1688320 | tf_op jit(solution)/shard_map/while/body/eval_jaxpr/...c,cj->...j/dot_general | solution.py:40
  118.2 1.3 fusion.48
  119.5 1.3 bitcast_compare_fusion.2
  121.7 1.8 %gather_fusion = f32[6,64,256]{2,1,0:T(8,128)S(1)} fusion(f32[16,64,256]{2,1,0:T(8,128)} %get-tuple-element.206, s32[1024]{0:T(1024)S(1)} %pad_clamp_fusion.2), kind=kCustom, calls=%fused_computation.1.clone.clone.1 | custom fusion | bytes 786456 | tf_op jit(solution)/shard_map/while/body/eval_jaxpr/jit(_take)/gather | solution.py:85
  124.6 1.9 %convolution_multiply_fusion.2 = f32[2,6,64,256]{3,2,1,0:T(8,128)S(1)} fusion(f32[1,6,68,276]{3,2,1,0:T(8,128)S(1)} %get-tuple-element.174, f32[1,6,68,276]{3,2,1,0:T(8,128)S(1)} %get-tuple-element.175, s32[256]{0:T(256)S(1)} %get-tuple-element.207), kind=kOutput, calls=%fused_computation.11.clone.1 | convolution fusion | flops 653552640 | bytes 1688320 | tf_op jit(solution)/shard_map/while/body/eval_jaxpr/...c,cj->...j/dot_general | solution.py:40
  130.0 1.3 fusion.48
  131.3 1.3 bitcast_compare_fusion.2
  133.5 1.8 %gather_fusion = f32[6,64,256]{2,1,0:T(8,128)S(1)} fusion(f32[16,64,256]{2,1,0:T(8,128)} %get-tuple-element.206, s32[1024]{0:T(1024)S(1)} %pad_clamp_fusion.2), kind=kCustom, calls=%fused_computation.1.clone.clone.1 | custom fusion | bytes 786456 | tf_op jit(solution)/shard_map/while/body/eval_jaxpr/jit(_take)/gather | solution.py:85
  136.3 1.9 %convolution_multiply_fusion.2 = f32[2,6,64,256]{3,2,1,0:T(8,128)S(1)} fusion(f32[1,6,68,276]{3,2,1,0:T(8,128)S(1)} %get-tuple-element.174, f32[1,6,68,276]{3,2,1,0:T(8,128)S(1)} %get-tuple-element.175, s32[256]{0:T(256)S(1)} %get-tuple-element.207), kind=kOutput, calls=%fused_computation.11.clone.1 | convolution fusion | flops 653552640 | bytes 1688320 | tf_op jit(solution)/shard_map/while/body/eval_jaxpr/...c,cj->...j/dot_general | solution.py:40
  141.7 1.3 fusion.48
  143.0 1.3 bitcast_compare_fusion.2
  145.3 1.8 %gather_fusion = f32[6,64,256]{2,1,0:T(8,128)S(1)} fusion(f32[16,64,256]{2,1,0:T(8,128)} %get-tuple-element.206, s32[1024]{0:T(1024)S(1)} %pad_clamp_fusion.2), kind=kCustom, calls=%fused_computation.1.clone.clone.1 | custom fusion | bytes 786456 | tf_op jit(solution)/shard_map/while/body/eval_jaxpr/jit(_take)/gather | solution.py:85
  148.1 1.9 %convolution_multiply_fusion.2 = f32[2,6,64,256]{3,2,1,0:T(8,128)S(1)} fusion(f32[1,6,68,276]{3,2,1,0:T(8,128)S(1)} %get-tuple-element.174, f32[1,6,68,276]{3,2,1,0:T(8,128)S(1)} %get-tuple-element.175, s32[256]{0:T(256)S(1)} %get-tuple-element.207), kind=kOutput, calls=%fused_computation.11.clone.1 | convolution fusion | flops 653552640 | bytes 1688320 | tf_op jit(solution)/shard_map/while/body/eval_jaxpr/...c,cj->...j/dot_general | solution.py:40
  151.0 1.9 %multiply_multiply_fusion = f32[8,64,256]{2,1,0:T(8,128)} fusion(f32[16,64,256]{2,1,0:T(8,128)} %fusion.33, f32[64,256]{1,0:T(8,128)S(1)} %convert_element_type.42), kind=kLoop, calls=%fused_computation.71 | loop fusion | flops 262144 | bytes 1114112 | tf_op jit(solution)/shard_map/div | solution.py:73
  (88 shorter events, 30.4 us)
Async XLA Ops:
  1.8 16.9 %collective-permute-start = (bf16[8,2,64,256]{3,2,0,1:T(8,128)(2,1)S(1)}, bf16[8,2,64,256]{3,2,0,1:T(8,128)(2,1)S(1)}, u32[]{:S(2)}, u32[]{:S(2)}) collective-permute-start(bf16[8,2,64,256]{3,2,0,1:T(8,128)(2,1)S(1)} %get-tuple-element.111), channel_id=1, source_target_pairs={{4,0},{8,4},{12,8},{5,1},{9,5},{13,9},{6,2},{10,6},{14,10},{7,3},{... | collective-permute-start | bytes 1572872 | tf_op jit(solution)/shard_map/ppermute | solution.py:16
  18.8 2.6 %collective-permute-start.1 = (bf16[16,2,2,256]{3,2,0,1:T(2,128)(2,1)S(1)}, bf16[16,2,2,256]{3,2,0,1:T(2,128)(2,1)S(1)}, u32[]{:S(2)}, u32[]{:S(2)}) collective-permute-start(bf16[16,2,2,256]{3,2,0,1:T(2,128)(2,1)S(1)} %get-tuple-element.109), channel_id=1, source_target_pairs={{0,1},{2,3},{4,5},{6,7},{8,9},{10,11},{12,13},{14,15},{16,17},{18,... | collective-permute-start | bytes 98312 | tf_op jit(solution)/shard_map/ppermute | solution.py:27
  20.1 3.1 %collective-permute-start.2 = (bf16[16,2,2,256]{3,2,0,1:T(2,128)(2,1)S(1)}, bf16[16,2,2,256]{3,2,0,1:T(2,128)(2,1)S(1)}, u32[]{:S(2)}, u32[]{:S(2)}) collective-permute-start(bf16[16,2,2,256]{3,2,0,1:T(2,128)(2,1)S(1)} %get-tuple-element.110), channel_id=1, source_target_pairs={{1,0},{3,2},{5,4},{7,6},{9,8},{11,10},{13,12},{15,14},{17,16},{19,... | collective-permute-start | bytes 98312 | tf_op jit(solution)/shard_map/ppermute | solution.py:29
  24.9 8.3 %collective-permute-start.4 = (bf16[16,2,68,10]{2,0,3,1:T(8,128)(2,1)S(1)}, bf16[16,2,68,10]{2,0,3,1:T(8,128)(2,1)S(1)}, u32[]{:S(2)}, u32[]{:S(2)}) collective-permute-start(bf16[16,2,68,10]{2,0,3,1:T(8,128)(2,1)S(1)} %copy.13), channel_id=1, source_target_pairs={{2,0},{3,1},{6,4},{7,5},{10,8},{11,9},{14,12},{15,13},{18,16},{19,... | collective-permute-start | bytes 130568 | tf_op jit(solution)/shard_map/ppermute | solution.py:29
  26.2 6.6 %collective-permute-start.3 = (bf16[16,2,68,10]{2,0,3,1:T(8,128)(2,1)S(1)}, bf16[16,2,68,10]{2,0,3,1:T(8,128)(2,1)S(1)}, u32[]{:S(2)}, u32[]{:S(2)}) collective-permute-start(bf16[16,2,68,10]{2,0,3,1:T(8,128)(2,1)S(1)} %copy.12), channel_id=1, source_target_pairs={{0,2},{1,3},{4,6},{5,7},{8,10},{9,11},{12,14},{13,15},{16,18},{17,... | collective-permute-start | bytes 130568 | tf_op jit(solution)/shard_map/ppermute | solution.py:27
where the time goes:
time: 155 us; the launch traced here: 153 us
  other arithmetic  37.6 us (24%)
  local copies, waits for them, and re-layouts  35.2 us (23%)
  waiting for transfers between devices  19.4 us (13%)
  matrix products  17.5 us (11%)
  blocking collectives  17.4 us (11%)
  loops' own time  15.3 us (10%)
  starting transfers between devices  9.72 us (6%)
    dot_general x9, matrix products, box_mean(): jnp.einsum('...c,cj->...j', row_sums, band_matrix, precision=lax.Precisio...  17.5 us
    psum x1, blocking collectives, on_device(): lax.psum(local_sum.astype(jnp.bfloat16), 'date').astype(jnp.float32)  17.4 us
    ppermute x1, waiting for transfers between devices, shifted(): return lax.ppermute(x, axis, pairs)  15.6 us
    another operation x1, loops' own time, on_device(): lax.map(one_date, (jnp.arange(date_count, dtype=jnp.int32), lags))  15.3 us
    gather x8, local copies, waits for them, and re-layouts, one_date(): partner_mean = jnp.take(mean_power, partners, axis=0)  14.4 us
    gt x8, other arithmetic, one_date(): live_slots = lag_row > 0  10.6 us
    select_n x8, other arithmetic, one_date(): second = jnp.take(tiles, partners, axis=0).astype(jnp.float32)  10.5 us
    dynamic_update_slice x8, other arithmetic, on_device(): lax.map(one_date, (jnp.arange(date_count, dtype=jnp.int32), lags))  8.02 us
  transfers between devices with their start and end apart: 5, of which 3 were waited for; matrix products, arithmetic and copies ran while one was open for 0% of the time, Pallas kernels for 0%

commit v1 on v0

v1 whole, which is shorter than its diff:
```python
import functools

import jax
import jax.numpy as jnp
from jax import lax
from jax.experimental import pallas as pl
from jax.experimental.pallas import tpu as pltpu
from jax.sharding import PartitionSpec as P

HALF_AZ = 2
HALF_RG = 10
LAG_MAX = 8
EPS = 1e-05
LOOKS = float((2 * HALF_AZ + 1) * (2 * HALF_RG + 1))

LANES = 128
ROWS = 16
AHEAD_Z = 5
AHEAD_X = 2
F32 = jnp.float32
BF16 = jnp.bfloat16


def gather_kernel(sizes, slc, coh_out, log_out, mean_out, total_out,
                  tiles, band, coh, logs, inv, mean, acc, total, chain_out, chain_in,
                  own_sem, z_send, z_recv, x_send, x_recv, a_send, a_recv,
                  c_send, c_recv, out_sem):
    dates_axis, rng_axis, dates, lines, cols = sizes
    sides = 1 if rng_axis == 2 else 2
    date = lax.axis_index("date")
    rng = lax.axis_index("rng")
    az = lax.axis_index("az")
    has_next = date < dates_axis - 1
    has_prev = date > 0
    has_right = rng < rng_axis - 1
    has_left = rng > 0
    peer = 1 - az
    center = (slice(None), pl.ds(0, lines), pl.ds(0, cols))

    own = pltpu.make_async_copy(
        slc, tiles.at[pl.ds(0, dates), :, pl.ds(0, lines), pl.ds(0, cols)], own_sem)
    own.start()

    barrier = pltpu.get_barrier_semaphore()

    def greet(where):
        pl.semaphore_signal(barrier, inc=1, device_id=where, device_id_type=pl.DeviceIdType.MESH)

    greet({"az": peer})
    pl.when(has_prev)(lambda: greet({"date": date - 1}))
    pl.when(has_next)(lambda: greet({"date": date + 1}))
    pl.when(has_left)(lambda: greet({"rng": rng - 1}))
    pl.when(has_right)(lambda: greet({"rng": rng + 1}))

    col_out = lax.broadcasted_iota(jnp.int32, (cols, cols), 1)
    col_in = lax.broadcasted_iota(jnp.int32, (cols, cols), 0)
    band[0:cols, :] = (jnp.abs(col_in - col_out) <= HALF_RG).astype(F32).astype(BF16)
    edge_in = lax.broadcasted_iota(jnp.int32, (LANES, cols), 0)
    edge_out = lax.broadcasted_iota(jnp.int32, (LANES, cols), 1)
    for side in range(sides):
        if sides == 1:
            shift = (1 - rng) * cols - rng * LANES
        else:
            shift = -LANES if side == 0 else cols
        near = jnp.abs(edge_in + shift - edge_out) <= HALF_RG
        band[cols + side * LANES:cols + (side + 1) * LANES, :] = near.astype(F32).astype(BF16)

    peers = 1
    for cond in (has_prev, has_next, has_left, has_right):
        peers = peers + cond.astype(jnp.int32)
    pl.semaphore_wait(barrier, peers)

    def x_copy(e, src, side, to, start_col):
        block = cols + side * LANES
        if not isinstance(start_col, int):
            start_col = pl.multiple_of(start_col, LANES)
        return pltpu.make_async_remote_copy(
            src_ref=src.at[:, pl.ds(0, lines), pl.ds(start_col, LANES)],
            dst_ref=tiles.at[e, :, pl.ds(0, lines), pl.ds(block, LANES)],
            send_sem=x_send.at[side, e], recv_sem=x_recv.at[side, e],
            device_id={"rng": to}, device_id_type=pl.DeviceIdType.MESH)

    def x_each(e, src, act):
        if sides == 1:
            act(x_copy(e, src, 0, 1 - rng, (1 - rng) * (cols - LANES)))
        else:
            pl.when(has_right)(lambda: act(x_copy(e, src, 0, rng + 1, cols - LANES)))
            pl.when(has_left)(lambda: act(x_copy(e, src, 1, rng - 1, 0)))

    def x_wait(e):
        src = tiles.at[e]
        if sides == 1:
            x_copy(e, src, 0, 1 - rng, 0).wait_recv()
        else:
            pl.when(has_left)(lambda: x_copy(e, src, 0, rng - 1, 0).wait_recv())
            pl.when(has_right)(lambda: x_copy(e, src, 1, rng + 1, 0).wait_recv())

    row_src = (1 - az) * (lines - ROWS)

    def a_copy(e):
        return pltpu.make_async_remote_copy(
            src_ref=tiles.at[e, :, pl.ds(pl.multiple_of(row_src, ROWS), ROWS), :],
            dst_ref=tiles.at[e, :, pl.ds(lines, ROWS), :],
            send_sem=a_send.at[e], recv_sem=a_recv.at[e],
            device_id={"az": peer}, device_id_type=pl.DeviceIdType.MESH)

    def z_copy(k, to):
        return pltpu.make_async_remote_copy(
            src_ref=slc.at[k], dst_ref=tiles.at[(dates + k, *center)],
            send_sem=z_send.at[k], recv_sem=z_recv.at[k],
            device_id={"date": to}, device_id_type=pl.DeviceIdType.MESH)

    for k in range(dates):
        x_each(k, slc.at[k], lambda c: c.start())

    @pl.when(has_prev)
    def _():
        for k in range(dates):
            z_copy(k, date - 1).start()

    if sides == 2:
        zeros = jnp.zeros((2 * dates, 2, lines, LANES), BF16)

        @pl.when(rng == 0)
        def _():
            tiles[:, :, 0:lines, cols:cols + LANES] = zeros

        @pl.when(rng == rng_axis - 1)
        def _():
            tiles[:, :, 0:lines, cols + LANES:cols + 2 * LANES] = zeros

    own.wait()

    top = az.astype(F32)
    bottom = 1.0 - top

    def line_sums(y):
        ext = jnp.concatenate(
            [y[lines + 8:lines + 16] * top, y[0:lines], y[lines:lines + 8] * bottom], axis=0)
        n = lines + 16
        two = ext + pltpu.roll(ext, n - 1, 0)
        five = pltpu.roll(two, 2, 0) + (ext + pltpu.roll(two, n - 1, 0))
        return five[8:8 + lines]

    height = lines + ROWS

    def powers_of(e):
        a0 = tiles[e, 0].astype(F32)
        a1 = tiles[e, 1].astype(F32)
        p = a0 * a0 + a1 * a1
        hi = p.astype(BF16)
        lo = (p - hi.astype(F32)).astype(BF16)
        y = jnp.dot(jnp.concatenate([hi, lo], axis=0), band[...], preferred_element_type=F32)
        m = line_sums(y[0:height] + y[height:]) * (1.0 / LOOKS) + EPS
        r = 1.0 / m
        logs[e] = jnp.log(m)
        inv[e] = r * (1.0 / LOOKS)
        if e < dates:
            mean[e] = m
            term = p[0:lines, 0:cols] * r
            if e == 0:
                acc[...] = term
            else:
                acc[...] += term

    def pairs_of(e, first, last):
        def one(d, carry):
            a0 = tiles[d, 0]
            a1 = tiles[d, 1]
            b0 = tiles[e, 0]
            b1 = tiles[e, 1]
            re = a0 * b0 + a1 * b1
            im = a1 * b0 - a0 * b1
            y = jnp.dot(jnp.concatenate([re, im], axis=0), band[...], preferred_element_type=F32)
            sr = line_sums(y[0:height])
            si = line_sums(y[height:])
            coh[e, e - d - 1] = ((sr * sr + si * si) * (inv[d] * inv[e])).astype(BF16)
            return carry
        lax.fori_loop(first, last, one, 0)

    def put(src, dst, i):
        return pltpu.make_async_copy(src, dst, out_sem.at[i])

    def puts(e):
        out = [put(logs.at[e], log_out.at[e], 3 * e)]
        lo, hi = (0, e) if e < dates else (e - dates, LAG_MAX)
        if hi > lo:
            out.append(put(coh.at[e, pl.ds(lo, hi - lo)], coh_out.at[e, pl.ds(lo, hi - lo)], 3 * e + 1))
        if e < dates:
            out.append(put(mean.at[e], mean_out.at[e], 3 * e + 2))
        return out

    def stage_z(e):
        z_copy(e - dates, date - 1).wait_recv()
        x_each(e, tiles.at[e], lambda c: c.start())

    def stage_x(e):
        x_wait(e)
        a_copy(e).start()

    def stage_c(e):
        a_copy(e).wait_recv()
        powers_of(e)
        if e < dates:
            pairs_of(e, 0, e)
        else:
            pairs_of(e, e - dates, dates)
        for c in puts(e):
            c.start()

    def chain(way, to):
        return pltpu.make_async_remote_copy(
            src_ref=chain_out.at[way], dst_ref=chain_in.at[way],
            send_sem=c_send.at[way], recv_sem=c_recv.at[way],
            device_id={"date": to}, device_id_type=pl.DeviceIdType.MESH)

    def up_step(first):
        if not first:
            chain(0, date + 1).wait_recv()

        @pl.when(has_next)
        def _():
            s = acc[...] if first else acc[...] + chain_in[0].astype(F32)
            chain_out[0] = s.astype(BF16)
            chain(0, date + 1).start()

    def down_step(first):
        if not first:
            chain(1, date - 1).wait_recv()

        @pl.when(has_prev)
        def _():
            s = acc[...] if first else acc[...] + chain_in[1].astype(F32)
            chain_out[1] = s.astype(BF16)
            chain(1, date - 1).start()

    def chain_point(k, rest):
        if rest:
            pl.when(date >= k)(lambda: up_step(False))
            pl.when(date <= dates_axis - 1 - k)(lambda: down_step(False))
        else:
            pl.when(date == k)(lambda: up_step(k == 0))
            pl.when(date == dates_axis - 1 - k)(lambda: down_step(k == 0))

    def stage(f, e):
        if e < 2 * dates:
            if e < dates:
                if f is not stage_z:
                    f(e)
            else:
                pl.when(has_next)(lambda: f(e))

    for e in range(AHEAD_Z):
        stage(stage_z, e)
    for e in range(AHEAD_X):
        stage(stage_x, e)
    points = [(dates - 1) + 2 * k for k in range(1 + dates // 2)]
    for e in range(2 * dates):
        stage(stage_z, e + AHEAD_Z)
        stage(stage_x, e + AHEAD_X)
        stage(stage_c, e)
        if e in points:
            k = points.index(e)
            if k < dates_axis:
                chain_point(k, k == len(points) - 1 and k < dates_axis - 1)

    total[...] = acc[...]

    @pl.when(has_prev)
    def _():
        total[...] += chain_in[0].astype(F32)

    @pl.when(has_next)
    def _():
        total[...] += chain_in[1].astype(F32)

    total[...] = total[...] * (1.0 / float(dates * dates_axis))
    last = put(total, total_out, 6 * dates)
    last.start()

    for e in range(2 * dates):
        def done(e=e):
            for c in puts(e):
                c.wait()
            x_each(e, tiles.at[e], lambda c: c.wait_send())
            a_copy(e).wait_send()
        if e < dates:
            done()
        else:
            pl.when(has_next)(done)

    @pl.when(has_prev)
    def _():
        for k in range(dates):
            z_copy(k, date - 1).wait_send()
        chain(1, date - 1).wait_send()

    @pl.when(has_next)
    def _():
        chain(0, date + 1).wait_send()

    last.wait()


def pick_kernel(sizes, lags, coh_in, log_in, mean_in, total_in, coh_out, log_out, queg_out,
                coh, logs, ratio, mean, total, in_sem, log_sem, mean_sem, out_sem):
    dates, slots, lines, cols = sizes
    tot = pltpu.make_async_copy(total_in, total, mean_sem.at[0])
    means = pltpu.make_async_copy(mean_in, mean, mean_sem.at[1])
    loads = pltpu.make_async_copy(log_in, logs, log_sem)

    def fetch(d, s):
        lag = jnp.maximum(lags[d, s], 1)
        return pltpu.make_async_copy(coh_in.at[d + lag, lag - 1], coh.at[d, s], in_sem.at[d])

    tot.start()
    means.start()
    loads.start()

    def start(d, carry):
        for s in range(slots):
            fetch(d, s).start()
        return carry

    lax.fori_loop(0, dates, start, 0)
    tot.wait()
    means.wait()

    def queg(d, carry):
        mean[d] = mean[d] * total[...]
        return carry

    lax.fori_loop(0, dates, queg, 0)
    pltpu.make_async_copy(mean, queg_out, out_sem.at[0]).start()
    loads.wait()

    def each(d, carry):
        for s in range(slots):
            lag = lags[d, s]

            @pl.when(lag > 0)
            def _():
                ratio[d, s] = (logs[d] - logs[d + lag]).astype(BF16)

            @pl.when(lag <= 0)
            def _():
                ratio[d, s] = jnp.zeros((lines, cols), BF16)
        pltpu.make_async_copy(ratio.at[d], log_out.at[d], out_sem.at[1]).start()
        for s in range(slots):
            fetch(d, s).wait()
        for s in range(slots):
            @pl.when(lags[d, s] <= 0)
            def _():
                coh[d, s] = jnp.zeros((lines, cols), BF16)
        pltpu.make_async_copy(coh.at[d], coh_out.at[d], out_sem.at[2]).start()
        return carry

    lax.fori_loop(0, dates, each, 0)
    pltpu.make_async_copy(mean, queg_out, out_sem.at[0]).wait()
    pltpu.make_async_copy(ratio, log_out, out_sem.at[1]).wait()
    pltpu.make_async_copy(coh, coh_out, out_sem.at[2]).wait()


def solution(mesh):
    dates_axis, rng_axis, az_axis = mesh.shape["date"], mesh.shape["rng"], mesh.shape["az"]
    assert az_axis == 2 and rng_axis > 1
    sides = 1 if rng_axis == 2 else 2

    def on_device(slc, lags):
        dates, _, lines, cols = slc.shape
        slots = lags.shape[1]
        assert dates == LAG_MAX
        width = cols + sides * LANES
        anywhere = pl.BlockSpec(memory_space=pl.ANY)
        field = (lines, cols)
        dma = pltpu.SemaphoreType.DMA
        coh, logs, mean, total = pl.pallas_call(
            functools.partial(gather_kernel, (dates_axis, rng_axis, dates, lines, cols)),
            out_shape=[
                jax.ShapeDtypeStruct((2 * dates, LAG_MAX, *field), BF16),
                jax.ShapeDtypeStruct((2 * dates, *field), F32),
                jax.ShapeDtypeStruct((dates, *field), F32),
                jax.ShapeDtypeStruct(field, F32),
            ],
            in_specs=[anywhere],
            out_specs=[anywhere] * 4,
            scratch_shapes=[
                pltpu.VMEM((2 * dates, 2, lines + ROWS, width), BF16),
                pltpu.VMEM((width, cols), BF16),
                pltpu.VMEM((2 * dates, LAG_MAX, *field), BF16),
                pltpu.VMEM((2 * dates, *field), F32),
                pltpu.VMEM((2 * dates, *field), F32),
                pltpu.VMEM((dates, *field), F32),
                pltpu.VMEM(field, F32),
                pltpu.VMEM(field, F32),
                pltpu.VMEM((2, *field), BF16),
                pltpu.VMEM((2, *field), BF16),
                dma, dma((dates,)), dma((dates,)),
                dma((sides, 2 * dates)), dma((sides, 2 * dates)),
                dma((2 * dates,)), dma((2 * dates,)),
                dma((2,)), dma((2,)), dma((6 * dates + 1,)),
            ],
            compiler_params=pltpu.CompilerParams(collective_id=0, has_side_effects=True),
            name="gather",
        )(slc)
        return pl.pallas_call(
            functools.partial(pick_kernel, (dates, slots, lines, cols)),
            out_shape=[
                jax.ShapeDtypeStruct((dates, slots, *field), BF16),
                jax.ShapeDtypeStruct((dates, slots, *field), BF16),
                jax.ShapeDtypeStruct((dates, *field), F32),
            ],
            in_specs=[pl.BlockSpec(memory_space=pltpu.SMEM)] + [anywhere] * 4,
            out_specs=[anywhere] * 3,
            scratch_shapes=[
                pltpu.VMEM((dates, slots, *field), BF16),
                pltpu.VMEM((2 * dates, *field), F32),
                pltpu.VMEM((dates, slots, *field), BF16),
                pltpu.VMEM((dates, *field), F32),
                pltpu.VMEM(field, F32),
                dma((dates,)), dma, dma((2,)), dma((3,)),
            ],
            name="pick",
        )(lags, coh, logs, mean, total)

    return jax.shard_map(
        on_device,
        mesh=mesh,
        in_specs=(P(("slab", "date"), None, "az", "rng"), P("date", None)),
        out_specs=(
            P(("slab", "date"), None, "az", "rng"),
            P(("slab", "date"), None, "az", "rng"),
            P(("slab", "date"), "az", "rng"),
        ),
        check_vma=False,
    )
```

time: 155 us -> 36.5 us (0.24); the launches traced: 153 us -> 36.3 us
  other arithmetic: 37.6 us -> 0 us
  Pallas kernels: 0 us -> 35.6 us
  local copies, waits for them, and re-layouts: 35.2 us -> 0 us
  waiting for transfers between devices: 19.4 us -> 0 us
  matrix products: 17.5 us -> 0 us
  blocking collectives: 17.4 us -> 0 us
  loops' own time: 15.3 us -> 0 us
  starting transfers between devices: 9.72 us -> 0 us
    pallas_call x0 -> x2, Pallas kernels: none -> 35.6 us  [the longest x1 31.1 us: on_device(): pl.pallas_call(functools.partial(gather_kernel, (dates_axis, rng_axis, da...]
    gather x16 -> x0, local copies, waits for them, and re-layouts: 20 us -> none  [the longest x8 14.4 us: one_date(): partner_mean = jnp.take(mean_power, partners, axis=0)]
    ppermute x5 -> x0, waiting for transfers between devices: 19.4 us -> none  [the longest x1 15.6 us: shifted(): return lax.ppermute(x, axis, pairs)]
    dot_general x9 -> x0, matrix products: 17.5 us -> none  [box_mean(): jnp.einsum('...c,cj->...j', row_sums, band_matrix, precision=lax.Precisio...]
    psum x1 -> x0, blocking collectives: 17.4 us -> none  [on_device(): lax.psum(local_sum.astype(jnp.bfloat16), 'date').astype(jnp.float32)]
    another operation x1 -> x0, loops' own time: 15.3 us -> none  [on_device(): lax.map(one_date, (jnp.arange(date_count, dtype=jnp.int32), lags))]
    gt x8 -> x0, other arithmetic: 10.6 us -> none  [one_date(): live_slots = lag_row > 0]
    select_n x8 -> x0, other arithmetic: 10.5 us -> none  [one_date(): second = jnp.take(tiles, partners, axis=0).astype(jnp.float32)]
  transfers between devices with their start and end apart: 5 -> 0, of which waited for: 3 -> 0; matrix products, arithmetic and copies ran while one was open for 0% -> 0% of each run, Pallas kernels for 0% -> 0%
where the time goes in v1:
time: 36.5 us; the launch traced here: 36.3 us
  Pallas kernels  35.6 us (98%)
  between operations  0.64 us (2%)
    pallas_call x1, Pallas kernels, on_device(): pl.pallas_call(functools.partial(gather_kernel, (dates_axis, rng_axis, da...  31.1 us
    pallas_call x1, Pallas kernels, on_device(): pl.pallas_call(functools.partial(pick_kernel, (dates, slots, lines, cols)...  4.52 us

profile of v1, /device:TPU:0, one launch (start us, length us, event | category | flops | bytes accessed | tf_op | source)
XLA Modules:
  0.0 36.3 jit_solution(2646601596294164677)
XLA Ops:
  0.6 31.1 %gather.1 = (bf16[16,8,64,256]{3,2,1,0:T(8,128)(2,1)}, f32[16,64,256]{2,1,0:T(8,128)}, f32[8,64,256]{2,1,0:T(8,128)}, f32[64,256]{1,0:T(8,128)}) custom-call(bf16[8,2,64,256]{3,2,1,0:T(8,128)(2,1)} %slc.1), custom_call_target="tpu_custom_call" | custom-call | tf_op jit(solution)/shard_map/gather/pallas_call | solution.py:377
  31.7 4.5 %pick.1 = (bf16[8,6,64,256]{3,2,1,0:T(8,128)(2,1)}, bf16[8,6,64,256]{3,2,1,0:T(8,128)(2,1)}, f32[8,64,256]{2,1,0:T(8,128)}) custom-call(s32[8,6]{1,0:T(8,128)} %lags.1, bf16[16,8,64,256]{3,2,1,0:T(8,128)(2,1)} %get-tuple-element.7.coh_in, f32[16,64,256]{2,1,0:T(8,128)} %get-tuple-element.8.log_in, f32[8,64,256]{2,1,0:T(8,128)} %get-tuple-element.9.mean_in, ...), custom_call_target="tpu_custom_call" | custom-call | tf_op jit(solution)/shard_map/pick/pallas_call | solution.py:406
